TPU v7x, 256 devices: a whole 4x4x8 slice. The times are simulated.
256 devices in a mesh: grp: 4 (over z_lo, core), fsdp: 64 (over z_hi, x, y).
Axes of the slice: x: 4, y: 4, z: 8 (z_hi: 4, z_lo: 2; z = z_hi * 2 + z_lo), core: 2. Of those that a mesh axis runs over, the one named last changes fastest.
Arguments:
- layer_input_rows: bfloat16 [131072, 8192], P(('grp', 'fsdp')), may hold values from -400 to 400, as said below
- input_norm_gain: bfloat16 [8192], replicated, may hold values from 0.5 to 1.5
- key_value_codes: int32 [8192, 256], P('fsdp'), may hold values from 0 to 65535
- block_scale_codes: int32 [256, 128], P('fsdp'), may hold values from -2147483648 to 2147483646
- outer_scale_codes: int32 [512], P('fsdp'), may hold values from 0 to 255
- adapter_down_factor: bfloat16 [8192, 64], replicated, may hold values from -0.0625 to 0.0625
- adapter_up_factor: bfloat16 [64, 1024], replicated, may hold values from -0.75 to 0.75
- target: bfloat16 [131072, 1024], P(('grp', 'fsdp')), may hold values from -18 to 18
Outputs:
- kv: bfloat16 [131072, 1024], P(('grp', 'fsdp'))
- loss: float32 [], replicated
Inputs may be any that keep to these rules, and one draw needn't show every extreme that they name: layer_input_rows rows and features carry varied scales.
All inputs are finite; a program needn't handle non-finite values.
Results may differ from a plain program's by a relative error of at most 0.0057.
Values may be sent and summed in bfloat16 or wider, within the bound.
No kernel may reach another device: no remote copies, remote signals or barrier semaphores. Data moves between devices by JAX's collectives and lax.ppermute only.
A program may use at most 128 MiB of HBM per device.

v0:
```python
import jax
import jax.numpy as jnp
from jax import lax
from jax.sharding import PartitionSpec as P

adapter_scale = 0.25
epsilon = 1e-06
nf4_levels = (
    -1.0,
    -0.6961928009986877,
    -0.5250730514526367,
    -0.39491748809814453,
    -0.28444138169288635,
    -0.18477343022823334,
    -0.09105003625154495,
    0.0,
    0.07958029955625534,
    0.16093020141124725,
    0.24611230194568634,
    0.33791524171066284,
    0.44070982933044434,
    0.5626170039176941,
    0.7229568362236023,
    1.0,
)


def copy_for_each(value, axis):
    length = lax.axis_size(axis)
    return lax.all_to_all(
        jnp.broadcast_to(value[None], (length, *value.shape)), axis, 0, 0, tiled=True
    )


def taken_together(value, axis):
    everything = copy_for_each(value, axis)
    return jnp.sum(everything, axis=0)


def unpack_scales(code_words, outer_scale_codes, all_rows):
    per_row = code_words.size // all_rows
    flat = code_words.reshape(all_rows, per_row)
    shifts = jnp.arange(4, dtype=jnp.int32) * 8
    code_bytes = jnp.bitwise_and(jnp.right_shift(flat[:, :, None], shifts[None, None, :]), 255)
    code_bytes = code_bytes.reshape(all_rows, per_row * 4).astype(jnp.float32)
    group_rows = all_rows // outer_scale_codes.shape[0]
    second = jnp.exp2(outer_scale_codes.astype(jnp.float32) / 128.0 - 6.0)
    second = jnp.repeat(second, group_rows)
    return (code_bytes + 0.5) / 256.0 * second[:, None]


def decode_codes(words, absmax):
    height = words.shape[0]
    shifts = jnp.arange(4, dtype=jnp.int32) * 4
    nibbles = jnp.bitwise_and(jnp.right_shift(words[:, :, None], shifts[None, None, :]), 15)
    nibbles = nibbles.reshape(height, words.shape[1] * 4)
    values = jnp.zeros(nibbles.shape, jnp.float32)
    for number, level in enumerate(nf4_levels):
        values = jnp.where(nibbles == number, jnp.float32(level), values)
    width = values.shape[1]
    count = absmax.shape[1]
    scaled = values.reshape(height, count, width // count) * absmax[:, :, None]
    return scaled.reshape(height, width).astype(jnp.bfloat16)


def apply_input_norm(input_states, input_norm_gain):
    values = input_states.astype(jnp.float32)
    inverse = lax.rsqrt(jnp.mean(values * values, axis=1, keepdims=True) + epsilon)
    return (values * inverse * input_norm_gain.astype(jnp.float32)[None, :]).astype(jnp.bfloat16)


def per_device(
    layer_input_rows,
    input_norm_gain,
    key_value_codes,
    block_scale_codes,
    outer_scale_codes,
    adapter_down_factor,
    adapter_up_factor,
    target,
):
    normed_input = apply_input_norm(layer_input_rows, input_norm_gain)
    rows_dev = key_value_codes.shape[0]
    columns = key_value_codes.shape[1] * 4
    owned = decode_codes(
        key_value_codes, unpack_scales(block_scale_codes, outer_scale_codes, rows_dev)
    )
    frozen_output = jnp.dot(
        normed_input,
        lax.all_gather(owned, "fsdp", axis=0, tiled=True),
        preferred_element_type=jnp.float32,
    )
    adapter_output = jnp.dot(
        normed_input, adapter_down_factor, preferred_element_type=jnp.float32
    ).astype(jnp.bfloat16)
    precise_output = frozen_output + adapter_scale * jnp.dot(
        adapter_output, adapter_up_factor, preferred_element_type=jnp.float32
    )
    error_terms = precise_output - target.astype(jnp.float32)
    partial_value = jnp.sum(error_terms * error_terms) / (
        normed_input.shape[0] * lax.axis_size("fsdp") * columns
    )
    group_total = taken_together(partial_value, "fsdp")
    loss = taken_together(group_total, "grp")
    return (precise_output.astype(jnp.bfloat16), loss)


def solution(mesh):
    placed = (
        P(("grp", "fsdp"), None),
        P(),
        P("fsdp", None),
        P("fsdp", None),
        P("fsdp"),
        P(),
        P(),
        P(("grp", "fsdp"), None),
    )
    return jax.shard_map(
        per_device,
        mesh=mesh,
        in_specs=placed,
        out_specs=(P(("grp", "fsdp"), None), P()),
        check_vma=False,
    )
```

profile of v0, /device:TPU:1, one launch (start us, length us, event | category | flops | bytes accessed | tf_op | source)
XLA Modules:
  0.0 304.2 jit_solution(3043209159881507789)
XLA Ops:
  7.2 0.0 copy-start
  7.2 0.0 copy-start.2
  7.2 0.0 all-gather.2.cloned.1.call-start
  7.3 0.7 exponential_multiply_fusion
  8.0 0.1 shift_right_arithmetic.58
  8.1 0.1 broadcast_in_dim.87
  8.2 0.1 mul.80
  8.2 0.8 shift_right_arithmetic.54
  9.0 0.1 copy.15
  9.1 0.1 shift_right_arithmetic.51
  9.3 1.0 copy.14
  10.3 0.1 add_multiply_fusion
  10.3 0.1 shift_right_arithmetic.48
  10.4 1.4 fusion.15
  11.8 0.0 all-gather.2.cloned.1.call-update
  11.9 0.7 convert_element_type.32
  12.6 5.1 %fusion = f32[512]{0:T(512)S(1)} fusion(bf16[512,8192]{1,0:T(8,128)(2,1)} %param.8), kind=kLoop, calls=%fused_computation.2 | loop fusion | flops 12582400 | bytes 8390656 | tf_op jit(solution)/shard_map/reduce_sum | solution.py:68
  17.7 0.0 copy-start.1
  17.7 0.0 copy-done
  17.7 0.0 copy-done.2
  17.7 7.9 %fusion.13 = f32[512,1024]{1,0:T(8,128)} fusion(bf16[64,1024]{1,0:T(8,128)(2,1)S(1)} %copy-done.2, bf16[8192,64]{0,1:T(8,128)(2,1)S(1)} %copy-done, bf16[512,8192]{1,0:T(8,128)(2,1)} %param.8, f32[8192]{0:T(1024)S(1)} %convert_element_type.32, f32[512]{0:T(512)S(1)} %add_rsqrt_fusion), kind=kOutput, calls=%fused_computation.10 | convolution fusion | flops 620789760 | bytes 11700224 | tf_op jit(solution)/shard_map/dot_general | solution.py:96
  25.6 223.1 %all-gather.2.cloned.1.call-done = bf16[8192,1024]{0,1:T(8,128)(2,1)} async-done(((bf16[128,1024]{0,1:T(8,128)(2,1)}), bf16[8192,1024]{0,1:T(8,128)(2,1)}) %all-gather.2.cloned.1.call-update) | async-done | bytes 16777232 | tf_op jit(solution)/shard_map/all_gather | solution.py:90
  248.7 0.0 copy-done.1
  248.7 16.8 %multiply_reduce_fusion = (f32[]{:T(128)}, bf16[512,1024]{1,0:T(8,128)(2,1)}) fusion(bf16[512,1024]{1,0:T(8,128)(2,1)S(1)} %copy-done.1, f32[512,1024]{1,0:T(8,128)} %fusion.13, bf16[8192,1024]{0,1:T(8,128)(2,1)} %all-gather.2.cloned.1.call-done, bf16[512,8192]{1,0:T(8,128)(2,1)} %param.8, f32[8192]{0:T(1024)S(1)} %convert_element_type.32, ...), kind=kOutput, calls=%fused_computation.7 | convolution fusion | flops 8610381824 | bytes 29394948 | tf_op jit(solution)/shard_map/dot_general | solution.py:88
  266.2 19.4 %all_to_all.12 = f32[64,1,1]{2,1,0:T(1,128)S(1)} all-to-all(f32[64,1,1]{2,1,0:T(1,128)S(1)} %broadcast_in_dim.88), channel_id=1, replica_groups=mesh['grp'=4,'fsdp'=64] {'fsdp'}, dimensions={0} | all-to-all | bytes 512 | tf_op jit(solution)/shard_map/all_to_all | solution.py:30
  285.5 0.7 reduce_sum.38
  286.2 0.6 broadcast_in_dim.89
  286.9 9.9 %all_to_all.13 = f32[4,1,1]{2,1,0:T(1,128)S(1)} all-to-all(f32[4,1,1]{2,1,0:T(1,128)S(1)} %broadcast_in_dim.89), channel_id=1, replica_groups=mesh['grp'=4,'fsdp'=64] {'grp'}, dimensions={0} | all-to-all | bytes 32 | tf_op jit(solution)/shard_map/all_to_all | solution.py:30
  296.7 0.6 reduce_sum.39
  (7 shorter events, 0.1 us)
Async XLA Ops:
  7.2 10.6 %copy-start = (bf16[8192,64]{0,1:T(8,128)(2,1)S(1)}, bf16[8192,64]{0,1:T(8,128)(2,1)}, u32[]{:S(2)}) copy-start(bf16[8192,64]{0,1:T(8,128)(2,1)} %param.13) | copy-start | bytes 3145732
  7.2 10.6 %copy-start.2 = (bf16[64,1024]{1,0:T(8,128)(2,1)S(1)}, bf16[64,1024]{1,0:T(8,128)(2,1)}, u32[]{:S(2)}) copy-start(bf16[64,1024]{1,0:T(8,128)(2,1)} %param.14) | copy-start | bytes 393220
  7.2 241.5 %all-gather.2.cloned.1.call-start = ((), (), s32[]{:S(2)}) async-start(), calls=%async_computation.2 | async-start | bytes 17039360 | tf_op jit(solution)/shard_map/all_gather | solution.py:90
  17.7 231.0 %copy-start.1 = (bf16[512,1024]{1,0:T(8,128)(2,1)S(1)}, bf16[512,1024]{1,0:T(8,128)(2,1)}, u32[]{:S(2)}) copy-start(bf16[512,1024]{1,0:T(8,128)(2,1)} %param.15) | copy-start | bytes 3145732
Sparse Core Ops, SparseCore 0:
  12.0 236.6 all-gather.1
where the time goes:
time: 304 us
  waiting for transfers between devices  223 us (73%)
  blocking collectives  29.2 us (10%)
  matrix products  24.7 us (8%)
  between operations  14.8 us (5%)
  other arithmetic  9.34 us (3%)
    all_gather x1, waiting for transfers between devices, per_device(): lax.all_gather(owned, 'fsdp', axis=0, tiled=True)  223 us
    all_to_all x2, blocking collectives, copy_for_each(): lax.all_to_all(jnp.broadcast_to(value[None], (length, *value.shape)), axi...  29.2 us
    dot_general x1, matrix products, per_device(): jnp.dot(normed_input, lax.all_gather(owned, 'fsdp', axis=0, tiled=True),...  16.8 us
    dot_general x1, matrix products, per_device(): jnp.dot(adapter_output, adapter_up_factor, preferred_element_type=jnp.flo...  7.88 us
  transfers between devices with their start and end apart: 1, of which 1 were waited for; matrix products, arithmetic and copies ran while one was open for 5% of the time, Pallas kernels for 0%

commit v1 on v0

--- a/solution.py
+++ b/solution.py
@@ -87,7 +87,9 @@
     )
     frozen_output = jnp.dot(
         normed_input,
-        lax.all_gather(owned, "fsdp", axis=0, tiled=True),
+        jnp.concatenate(
+            lax.all_to_all(jnp.stack([owned] * lax.axis_size("fsdp")), "fsdp", 0, 0), axis=0
+        ),
         preferred_element_type=jnp.float32,
     )
     adapter_output = jnp.dot(

time: 304 us -> 476 us (1.57)
  waiting for transfers between devices: 223 us -> 360 us
  blocking collectives: 29.2 us -> 56.7 us
  starting transfers between devices: 0.04 us -> 15.5 us
  between operations: 14.8 us -> 1.44 us
  local copies, waits for them, and re-layouts: 3 us -> 9.13 us
    all_to_all x0 -> x1, waiting for transfers between devices: none -> 360 us  [per_device(): lax.all_to_all(jnp.stack([owned] * lax.axis_size('fsdp')), 'fsdp', 0, 0)]
    all_gather x1 -> x0, waiting for transfers between devices: 223 us -> none  [per_device(): lax.all_gather(owned, 'fsdp', axis=0, tiled=True)]
    all_to_all x2, blocking collectives: 29.2 us -> 56.7 us  [copy_for_each(): lax.all_to_all(jnp.broadcast_to(value[None], (length, *value.shape)), axi...]
    all_to_all x0 -> x1, starting transfers between devices: none -> 15.5 us  [per_device(): lax.all_to_all(jnp.stack([owned] * lax.axis_size('fsdp')), 'fsdp', 0, 0)]
    another operation x0 -> x1, local copies, waits for them, and re-layouts: none -> 5.98 us  [per_device(): jnp.stack([owned] * lax.axis_size('fsdp'))]
  transfers between devices with their start and end apart: 1 -> 1, of which waited for: 1 -> 1; matrix products, arithmetic and copies ran while one was open for 5% -> 3% of each run, Pallas kernels for 0% -> 0%
where the time goes in v1:
time: 476 us; the launch traced here: 475 us
  waiting for transfers between devices  360 us (76%)
  blocking collectives  56.7 us (12%)
  matrix products  24.7 us (5%)
  starting transfers between devices  15.5 us (3%)
  local copies, waits for them, and re-layouts  9.13 us (2%)
  other arithmetic  7.99 us (2%)
    all_to_all x1, waiting for transfers between devices, per_device(): lax.all_to_all(jnp.stack([owned] * lax.axis_size('fsdp')), 'fsdp', 0, 0)  360 us
    all_to_all x2, blocking collectives, copy_for_each(): lax.all_to_all(jnp.broadcast_to(value[None], (length, *value.shape)), axi...  56.7 us
    dot_general x1, matrix products, per_device(): jnp.dot(normed_input, jnp.concatenate(lax.all_to_all(jnp.stack([owned] *...  16.8 us
    all_to_all x1, starting transfers between devices, per_device(): lax.all_to_all(jnp.stack([owned] * lax.axis_size('fsdp')), 'fsdp', 0, 0)  15.5 us
  transfers between devices with their start and end apart: 1, of which 1 were waited for; matrix products, arithmetic and copies ran while one was open for 3% of the time, Pallas kernels for 0%

profile of v1, /device:TPU:1, one launch (start us, length us, event | category | flops | bytes accessed | tf_op | source)
XLA Modules:
  0.0 475.2 jit_solution(5822764584704511812)
XLA Ops:
  0.6 0.0 copy-start
  0.7 0.7 exponential_multiply_fusion
  1.4 0.1 shift_right_arithmetic.60
  1.5 0.1 broadcast_in_dim.87
  1.6 0.1 mul.82
  1.7 0.8 shift_right_arithmetic.56
  2.5 0.1 copy.17
  2.5 0.1 shift_right_arithmetic.53
  2.7 1.0 copy.16
  3.7 0.1 add_multiply_fusion
  3.8 0.1 shift_right_arithmetic.50
  3.9 0.7 fusion.15
  4.6 0.1 copy.18
  4.7 6.0 %stack.2 = bf16[64,128,1024]{2,1,0:T(8,128)(2,1)} broadcast(bf16[128,1024]{1,0:T(8,128)(2,1)S(1)} %copy.18), dimensions={1,2} | broadcast | bytes 17039360 | tf_op jit(solution)/shard_map/stack | solution.py:91
  10.7 0.0 copy-start.1
  10.7 15.5 %all-to-all-start = ((bf16[64,128,1024]{2,1,0:T(8,128)(2,1)}), bf16[64,128,1024]{2,1,0:T(8,128)(2,1)}, u32[]{:S(2)}, u32[]{:S(2)}) async-start(bf16[64,128,1024]{2,1,0:T(8,128)(2,1)} %stack.2), calls=%async_computation | async-start | bytes 33554432 | tf_op jit(solution)/shard_map/all_to_all | solution.py:91
  26.2 0.0 copy-done.1
  26.3 0.0 copy-start.3
  26.3 5.1 %fusion = f32[512]{0:T(512)S(1)} fusion(bf16[512,8192]{1,0:T(8,128)(2,1)} %param.8), kind=kLoop, calls=%fused_computation.2 | loop fusion | flops 12582400 | bytes 8390656 | tf_op jit(solution)/shard_map/reduce_sum | solution.py:68
  31.4 0.0 copy-start.2
  31.4 0.0 copy-done
  31.4 0.0 copy-done.3
  31.5 7.8 %fusion.13 = f32[512,1024]{1,0:T(8,128)} fusion(bf16[64,1024]{1,0:T(8,128)(2,1)S(1)} %copy-done.3, bf16[8192,64]{0,1:T(8,128)(2,1)S(1)} %copy-done, bf16[512,8192]{1,0:T(8,128)(2,1)} %param.8, f32[8192]{0:T(1024)S(1)} %convert_element_type.34, f32[512]{0:T(512)S(1)} %add_rsqrt_fusion), kind=kOutput, calls=%fused_computation.10 | convolution fusion | flops 620789760 | bytes 11700224 | tf_op jit(solution)/shard_map/dot_general | solution.py:98
  39.3 359.7 %all-to-all-done = bf16[64,128,1024]{2,1,0:T(8,128)(2,1)} async-done(((bf16[64,128,1024]{2,1,0:T(8,128)(2,1)}), bf16[64,128,1024]{2,1,0:T(8,128)(2,1)}, u32[]{:S(2)}, u32[]{:S(2)}) %all-to-all-start) | async-done | bytes 16777248 | tf_op jit(solution)/shard_map/all_to_all | solution.py:91
  399.1 0.0 copy-done.2
  399.1 16.8 %multiply_reduce_fusion = (f32[]{:T(128)}, bf16[512,1024]{1,0:T(8,128)(2,1)}) fusion(bf16[512,1024]{1,0:T(8,128)(2,1)S(1)} %copy-done.2, f32[512,1024]{1,0:T(8,128)} %fusion.13, bf16[8192,1024]{1,0:T(8,128)(2,1)} %bitcast.3, bf16[512,8192]{1,0:T(8,128)(2,1)} %param.8, f32[8192]{0:T(1024)S(1)} %convert_element_type.34, f32[512]{0:T(512)S(1)} %add_rsqrt_fusion), kind=kOutput, calls=%fused_computation.7 | convolution fusion | flops 8610381824 | bytes 29394948 | tf_op jit(solution)/shard_map/dot_general | solution.py:88
  416.6 32.1 %all_to_all.17 = f32[64,1,1]{2,1,0:T(1,128)S(1)} all-to-all(f32[64,1,1]{2,1,0:T(1,128)S(1)} %broadcast_in_dim.88), channel_id=1, replica_groups=mesh['grp'=4,'fsdp'=64] {'fsdp'}, dimensions={0} | all-to-all | bytes 512 | tf_op jit(solution)/shard_map/all_to_all | solution.py:30
  448.7 0.7 reduce_sum.38
  449.3 0.6 broadcast_in_dim.89
  450.0 24.6 %all_to_all.18 = f32[4,1,1]{2,1,0:T(1,128)S(1)} all-to-all(f32[4,1,1]{2,1,0:T(1,128)S(1)} %broadcast_in_dim.89), channel_id=1, replica_groups=mesh['grp'=4,'fsdp'=64] {'grp'}, dimensions={0} | all-to-all | bytes 32 | tf_op jit(solution)/shard_map/all_to_all | solution.py:30
  474.6 0.6 reduce_sum.39
  (8 shorter events, 0.1 us)
Async XLA Ops:
  0.6 30.8 %copy-start = (bf16[8192,64]{0,1:T(8,128)(2,1)S(1)}, bf16[8192,64]{0,1:T(8,128)(2,1)}, u32[]{:S(2)}) copy-start(bf16[8192,64]{0,1:T(8,128)(2,1)} %param.13) | copy-start | bytes 3145732
  10.7 15.5 %copy-start.1 = (bf16[8192]{0:T(1024)(128)(2,1)S(1)}, bf16[8192]{0:T(1024)(128)(2,1)}, u32[]{:S(2)}) copy-start(bf16[8192]{0:T(1024)(128)(2,1)} %param.9) | copy-start | bytes 49156
  10.7 388.3 %all-to-all-start = ((bf16[64,128,1024]{2,1,0:T(8,128)(2,1)}), bf16[64,128,1024]{2,1,0:T(8,128)(2,1)}, u32[]{:S(2)}, u32[]{:S(2)}) async-start(bf16[64,128,1024]{2,1,0:T(8,128)(2,1)} %stack.2), calls=%async_computation | async-start | bytes 33554432 | tf_op jit(solution)/shard_map/all_to_all | solution.py:91
  26.3 5.2 %copy-start.3 = (bf16[64,1024]{1,0:T(8,128)(2,1)S(1)}, bf16[64,1024]{1,0:T(8,128)(2,1)}, u32[]{:S(2)}) copy-start(bf16[64,1024]{1,0:T(8,128)(2,1)} %param.14) | copy-start | bytes 393220
  31.4 367.6 %copy-start.2 = (bf16[512,1024]{1,0:T(8,128)(2,1)S(1)}, bf16[512,1024]{1,0:T(8,128)(2,1)}, u32[]{:S(2)}) copy-start(bf16[512,1024]{1,0:T(8,128)(2,1)} %param.15) | copy-start | bytes 3145732
